TPU v7x, 512 devices: a whole 4x4x16 slice. The times are simulated.
512 devices in a mesh: tm: 16 (over z_hi, y), lat: 32 (over x, z_lo, core).
Axes of the slice: x: 4, y: 4, z: 16 (z_hi: 4, z_lo: 4; z = z_hi * 4 + z_lo), core: 2. Of those that a mesh axis runs over, the one named last changes fastest.
Arguments:
- cotangent: float32 [64, 512, 2048], P('tm', 'lat'), may hold values from -6 to 6
- iterates: float32 [3, 64, 512, 2048], P(None, 'tm', 'lat'), may hold values from -6 to 6
- range_field: float32 [512, 2048], P('lat', 'tm'), may hold values from 0.05 to 1
Outputs:
- noise_cotangent: float32 [64, 512, 2048], P('tm', 'lat')
- range_gradient: float32 [512, 2048], P('lat', 'tm')
All inputs are finite; a program needn't handle non-finite values.
Results may differ from a plain program's by a relative error of at most 0.0001.
Values sent between devices are 32-bit elements; how exact they have to be, the bound alone decides.
A program may use at most 64 MiB of HBM per device.

v0:
```python
import math

import jax
import jax.numpy as jnp
from jax import lax
from jax.sharding import PartitionSpec as P


def extended(cells, sides, width):
    for axis, dim in sides:
        count = lax.axis_size(axis)
        ends = count - 1
        head = lax.slice_in_dim(cells, 0, width, axis=dim)
        tail = lax.slice_in_dim(cells, cells.shape[dim] - width, cells.shape[dim], axis=dim)
        cells = jnp.concatenate(
            [
                lax.ppermute(tail, axis, [(i, (i + 1) % count) for i in range(ends)]),
                cells,
                lax.ppermute(head, axis, [((i + 1) % count, i) for i in range(ends)]),
            ],
            axis=dim,
        )
    return cells


def step_weights():
    centre_value = 6.525
    spread_value = 6.475
    root_order = (3, 0, 2, 1)
    return [
        1.0 / (centre_value + spread_value * math.cos(math.pi * (2 * section + 1) / 8.0))
        for section in root_order
    ]


def stencil(field, coefficient, previous, following, upper_row, lower_row):
    longitude = jnp.roll(field, 1, 2) + jnp.roll(field, -1, 2)
    return (
        (coefficient[None, :, :] + 6.0) * field
        - upper_row
        - lower_row
        - longitude
        - previous
        - following
    )


def body(cotangent, iterates, range_field):
    weights = step_weights()
    range_rows = lax.all_gather(range_field, "tm", axis=1, tiled=True)
    adjoint = cotangent
    noise_cot = weights[3] * cotangent
    gradient = jnp.zeros(range_field.shape, jnp.float32)
    for section in (3, 2, 1):
        own_cells = adjoint
        product_sum = -weights[section] * jnp.sum(own_cells * iterates[section - 1], axis=0)
        gradient = gradient + lax.psum_scatter(product_sum, "tm", scatter_dimension=1, tiled=True)
        timed = extended(adjoint, (("tm", 0),), 1)
        rowed = extended(adjoint, (("lat", 1),), 1)
        applied = stencil(adjoint, range_rows, timed[:-2], timed[2:], rowed[:, 2:], rowed[:, :-2])
        adjoint = adjoint - weights[section] * applied
        noise_cot = noise_cot + weights[section - 1] * adjoint
    return (noise_cot, gradient)


def solution(mesh):
    placed = (P("tm", "lat", None), P(None, "tm", "lat", None), P("lat", "tm"))
    return jax.shard_map(
        body,
        mesh=mesh,
        in_specs=placed,
        out_specs=(P("tm", "lat", None), P("lat", "tm")),
        check_vma=False,
    )
```

profile of v0, /device:TPU:6, one launch (start us, length us, event | category | flops | bytes accessed | tf_op | source)
XLA Modules:
  0.0 247.5 jit_solution(584649050877484398)
XLA Ops:
  7.2 0.0 reduce-scatter.2.cloned.1.call-start
  7.2 1.1 fusion.37
  8.4 6.2 %collective-permute-start = (f32[4,1,2048]{2,1,0:T(1,128)S(1)}, f32[4,1,2048]{2,1,0:T(1,128)S(1)}, u32[]{:S(2)}, u32[]{:S(2)}) collective-permute-start(f32[4,1,2048]{2,1,0:T(1,128)S(1)} %get-tuple-element.26), channel_id=1, source_target_pairs={{1,0},{2,1},{3,2},{4,3},{5,4},{6,5},{7,6},{8,7},{9,8},{10,9},{11,1... | collective-permute-start | bytes 98312 | tf_op jit(solution)/shard_map/ppermute | solution.py:19
  14.6 1.9 collective-permute-start.1
  16.5 1.0 fusion.38
  17.5 3.5 %collective-permute-start.2 = (f32[1,16,2048]{2,1,0:T(8,128)S(1)}, f32[1,16,2048]{2,1,0:T(8,128)S(1)}, u32[]{:S(2)}, u32[]{:S(2)}) collective-permute-start(f32[1,16,2048]{2,1,0:T(8,128)S(1)} %get-tuple-element.28), channel_id=1, source_target_pairs={{0,32},{32,64},{64,96},{96,128},{128,160},{160,192},{192,224},{224... | collective-permute-start | bytes 393224 | tf_op jit(solution)/shard_map/ppermute | solution.py:17
  21.0 1.3 collective-permute-start.3
  22.3 1.4 fusion.35
  23.7 57.7 %all_gather.3 = f32[16,2048]{1,0:T(8,128)S(1)} all-gather(f32[16,128]{1,0:T(8,128)S(1)} %copy-done.2), channel_id=1, replica_groups=mesh['tm'=16,'lat'=32] {'tm'}, dimensions={1}, use_global_device_ids=true | all-gather | bytes 139264 | tf_op jit(solution)/shard_map/all_gather | solution.py:50
  81.4 0.1 fusion.36
  81.5 0.3 fusion.18
  82.0 0.2 fusion.33
  82.2 2.0 collective-permute-start.4
  84.2 2.4 collective-permute-start.5
  86.7 1.3 collective-permute-start.6
  88.0 1.3 collective-permute-start.7
  89.3 0.1 fusion.32
  89.3 2.8 %collective-permute-done.5 = f32[4,1,2048]{2,1,0:T(1,128)S(1)} collective-permute-done((f32[4,1,2048]{2,1,0:T(1,128)S(1)}, f32[4,1,2048]{2,1,0:T(1,128)S(1)}, u32[]{:S(2)}, u32[]{:S(2)}) %collective-permute-start.5) | collective-permute-done | bytes 32800 | tf_op jit(solution)/shard_map/ppermute | solution.py:17
  92.2 3.1 %collective-permute-done.7 = f32[1,16,2048]{2,1,0:T(8,128)S(1)} collective-permute-done((f32[1,16,2048]{2,1,0:T(8,128)S(1)}, f32[1,16,2048]{2,1,0:T(8,128)S(1)}, u32[]{:S(2)}, u32[]{:S(2)}) %collective-permute-start.7) | collective-permute-done | bytes 131104 | tf_op jit(solution)/shard_map/ppermute | solution.py:19
  95.3 0.5 fusion.25
  95.9 0.2 fusion.27
  96.1 4.3 %collective-permute-start.8 = (f32[4,1,2048]{2,1,0:T(1,128)S(1)}, f32[4,1,2048]{2,1,0:T(1,128)S(1)}, u32[]{:S(2)}, u32[]{:S(2)}) collective-permute-start(f32[4,1,2048]{2,1,0:T(1,128)S(1)} %get-tuple-element.10), channel_id=1, source_target_pairs={{1,0},{2,1},{3,2},{4,3},{5,4},{6,5},{7,6},{8,7},{9,8},{10,9},{11,1... | collective-permute-start | bytes 98312 | tf_op jit(solution)/shard_map/ppermute | solution.py:19
  100.3 1.9 collective-permute-start.9
  102.3 5.2 %collective-permute-start.10 = (f32[1,16,2048]{2,1,0:T(8,128)S(1)}, f32[1,16,2048]{2,1,0:T(8,128)S(1)}, u32[]{:S(2)}, u32[]{:S(2)}) collective-permute-start(f32[1,16,2048]{2,1,0:T(8,128)S(1)} %get-tuple-element.12), channel_id=1, source_target_pairs={{0,32},{32,64},{64,96},{96,128},{128,160},{160,192},{192,224},{224... | collective-permute-start | bytes 393224 | tf_op jit(solution)/shard_map/ppermute | solution.py:17
  107.5 1.3 collective-permute-start.11
  108.8 0.7 add_add_fusion
  109.5 0.1 fusion.28
  109.5 0.0 reduce-scatter.2.cloned.1.call-update
  109.6 4.3 %collective-permute-done.9 = f32[4,1,2048]{2,1,0:T(1,128)S(1)} collective-permute-done((f32[4,1,2048]{2,1,0:T(1,128)S(1)}, f32[4,1,2048]{2,1,0:T(1,128)S(1)}, u32[]{:S(2)}, u32[]{:S(2)}) %collective-permute-start.9) | collective-permute-done | bytes 32800 | tf_op jit(solution)/shard_map/ppermute | solution.py:17
  113.9 6.7 %collective-permute-done.11 = f32[1,16,2048]{2,1,0:T(8,128)S(1)} collective-permute-done((f32[1,16,2048]{2,1,0:T(8,128)S(1)}, f32[1,16,2048]{2,1,0:T(8,128)S(1)}, u32[]{:S(2)}, u32[]{:S(2)}) %collective-permute-start.11) | collective-permute-done | bytes 131104 | tf_op jit(solution)/shard_map/ppermute | solution.py:19
  120.6 1.2 fusion.4
  121.8 118.8 %reduce-scatter.2.cloned.1.call-done = f32[16,128]{1,0:T(8,128)} async-done(((f32[16,2048]{1,0:T(8,128)}), f32[16,128]{1,0:T(8,128)}) %reduce-scatter.2.cloned.1.call-update) | async-done | bytes 8208 | tf_op jit(solution)/shard_map/reduce_scatter | solution.py:57
  (19 shorter events, 0.2 us)
Async XLA Ops:
  7.2 74.3 %copy-start = (f32[4,16,2048]{2,1,0:T(8,128)S(1)}, f32[4,16,2048]{2,1,0:T(8,128)}, u32[]{:S(2)}) copy-start(f32[4,16,2048]{2,1,0:T(8,128)} %param.3) | copy-start | bytes 1572868
  7.2 16.6 %copy-start.2 = (f32[16,128]{1,0:T(8,128)S(1)}, f32[16,128]{1,0:T(8,128)}, u32[]{:S(2)}) copy-start(f32[16,128]{1,0:T(8,128)} %param.5) | copy-start | bytes 24580
  7.2 233.5 %reduce-scatter.2.cloned.1.call-start = ((), (), s32[]{:S(2)}) async-start(), calls=%async_computation.1 | async-start | bytes 139264 | tf_op jit(solution)/shard_map/reduce_scatter | solution.py:57
  8.4 73.2 %collective-permute-start = (f32[4,1,2048]{2,1,0:T(1,128)S(1)}, f32[4,1,2048]{2,1,0:T(1,128)S(1)}, u32[]{:S(2)}, u32[]{:S(2)}) collective-permute-start(f32[4,1,2048]{2,1,0:T(1,128)S(1)} %get-tuple-element.26), channel_id=1, source_target_pairs={{1,0},{2,1},{3,2},{4,3},{5,4},{6,5},{7,6},{8,7},{9,8},{10,9},{11,1... | collective-permute-start | bytes 98312 | tf_op jit(solution)/shard_map/ppermute | solution.py:19
  14.6 66.9 %collective-permute-start.1 = (f32[4,1,2048]{2,1,0:T(1,128)S(1)}, f32[4,1,2048]{2,1,0:T(1,128)S(1)}, u32[]{:S(2)}, u32[]{:S(2)}) collective-permute-start(f32[4,1,2048]{2,1,0:T(1,128)S(1)} %get-tuple-element.27), channel_id=1, source_target_pairs={{0,1},{1,2},{2,3},{3,4},{4,5},{5,6},{6,7},{7,8},{8,9},{9,10},{10,1... | collective-permute-start | bytes 98312 | tf_op jit(solution)/shard_map/ppermute | solution.py:17
  17.5 64.0 %collective-permute-start.2 = (f32[1,16,2048]{2,1,0:T(8,128)S(1)}, f32[1,16,2048]{2,1,0:T(8,128)S(1)}, u32[]{:S(2)}, u32[]{:S(2)}) collective-permute-start(f32[1,16,2048]{2,1,0:T(8,128)S(1)} %get-tuple-element.28), channel_id=1, source_target_pairs={{0,32},{32,64},{64,96},{96,128},{128,160},{160,192},{192,224},{224... | collective-permute-start | bytes 393224 | tf_op jit(solution)/shard_map/ppermute | solution.py:17
  21.0 60.5 %collective-permute-start.3 = (f32[1,16,2048]{2,1,0:T(8,128)S(1)}, f32[1,16,2048]{2,1,0:T(8,128)S(1)}, u32[]{:S(2)}, u32[]{:S(2)}) collective-permute-start(f32[1,16,2048]{2,1,0:T(8,128)S(1)} %get-tuple-element.29), channel_id=1, source_target_pairs={{32,0},{64,32},{96,64},{128,96},{160,128},{192,160},{224,192},{256... | collective-permute-start | bytes 393224 | tf_op jit(solution)/shard_map/ppermute | solution.py:19
  81.9 13.4 %copy-start.1 = (f32[3,4,16,2048]{3,2,1,0:T(8,128)S(1)}, f32[3,4,16,2048]{3,2,1,0:T(8,128)}, u32[]{:S(2)}) copy-start(f32[3,4,16,2048]{3,2,1,0:T(8,128)} %param.4) | copy-start | bytes 4718596
  82.2 7.2 %collective-permute-start.4 = (f32[4,1,2048]{2,1,0:T(1,128)S(1)}, f32[4,1,2048]{2,1,0:T(1,128)S(1)}, u32[]{:S(2)}, u32[]{:S(2)}) collective-permute-start(f32[4,1,2048]{2,1,0:T(1,128)S(1)} %get-tuple-element.14), channel_id=1, source_target_pairs={{1,0},{2,1},{3,2},{4,3},{5,4},{6,5},{7,6},{8,7},{9,8},{10,9},{11,1... | collective-permute-start | bytes 98312 | tf_op jit(solution)/shard_map/ppermute | solution.py:19
  84.2 7.9 %collective-permute-start.5 = (f32[4,1,2048]{2,1,0:T(1,128)S(1)}, f32[4,1,2048]{2,1,0:T(1,128)S(1)}, u32[]{:S(2)}, u32[]{:S(2)}) collective-permute-start(f32[4,1,2048]{2,1,0:T(1,128)S(1)} %get-tuple-element.15), channel_id=1, source_target_pairs={{0,1},{1,2},{2,3},{3,4},{4,5},{5,6},{6,7},{7,8},{8,9},{9,10},{10,1... | collective-permute-start | bytes 98312 | tf_op jit(solution)/shard_map/ppermute | solution.py:17
  86.7 5.5 %collective-permute-start.6 = (f32[1,16,2048]{2,1,0:T(8,128)S(1)}, f32[1,16,2048]{2,1,0:T(8,128)S(1)}, u32[]{:S(2)}, u32[]{:S(2)}) collective-permute-start(f32[1,16,2048]{2,1,0:T(8,128)S(1)} %get-tuple-element.20), channel_id=1, source_target_pairs={{0,32},{32,64},{64,96},{96,128},{128,160},{160,192},{192,224},{224... | collective-permute-start | bytes 393224 | tf_op jit(solution)/shard_map/ppermute | solution.py:17
  88.0 7.3 %collective-permute-start.7 = (f32[1,16,2048]{2,1,0:T(8,128)S(1)}, f32[1,16,2048]{2,1,0:T(8,128)S(1)}, u32[]{:S(2)}, u32[]{:S(2)}) collective-permute-start(f32[1,16,2048]{2,1,0:T(8,128)S(1)} %get-tuple-element.21), channel_id=1, source_target_pairs={{32,0},{64,32},{96,64},{128,96},{160,128},{192,160},{224,192},{256... | collective-permute-start | bytes 393224 | tf_op jit(solution)/shard_map/ppermute | solution.py:19
  96.1 13.5 %collective-permute-start.8 = (f32[4,1,2048]{2,1,0:T(1,128)S(1)}, f32[4,1,2048]{2,1,0:T(1,128)S(1)}, u32[]{:S(2)}, u32[]{:S(2)}) collective-permute-start(f32[4,1,2048]{2,1,0:T(1,128)S(1)} %get-tuple-element.10), channel_id=1, source_target_pairs={{1,0},{2,1},{3,2},{4,3},{5,4},{6,5},{7,6},{8,7},{9,8},{10,9},{11,1... | collective-permute-start | bytes 98312 | tf_op jit(solution)/shard_map/ppermute | solution.py:19
  100.3 13.6 %collective-permute-start.9 = (f32[4,1,2048]{2,1,0:T(1,128)S(1)}, f32[4,1,2048]{2,1,0:T(1,128)S(1)}, u32[]{:S(2)}, u32[]{:S(2)}) collective-permute-start(f32[4,1,2048]{2,1,0:T(1,128)S(1)} %get-tuple-element.11), channel_id=1, source_target_pairs={{0,1},{1,2},{2,3},{3,4},{4,5},{5,6},{6,7},{7,8},{8,9},{9,10},{10,1... | collective-permute-start | bytes 98312 | tf_op jit(solution)/shard_map/ppermute | solution.py:17
  102.3 11.7 %collective-permute-start.10 = (f32[1,16,2048]{2,1,0:T(8,128)S(1)}, f32[1,16,2048]{2,1,0:T(8,128)S(1)}, u32[]{:S(2)}, u32[]{:S(2)}) collective-permute-start(f32[1,16,2048]{2,1,0:T(8,128)S(1)} %get-tuple-element.12), channel_id=1, source_target_pairs={{0,32},{32,64},{64,96},{96,128},{128,160},{160,192},{192,224},{224... | collective-permute-start | bytes 393224 | tf_op jit(solution)/shard_map/ppermute | solution.py:17
  107.5 13.1 %collective-permute-start.11 = (f32[1,16,2048]{2,1,0:T(8,128)S(1)}, f32[1,16,2048]{2,1,0:T(8,128)S(1)}, u32[]{:S(2)}, u32[]{:S(2)}) collective-permute-start(f32[1,16,2048]{2,1,0:T(8,128)S(1)} %get-tuple-element.13), channel_id=1, source_target_pairs={{32,0},{64,32},{96,64},{128,96},{160,128},{192,160},{224,192},{256... | collective-permute-start | bytes 393224 | tf_op jit(solution)/shard_map/ppermute | solution.py:19
Sparse Core Ops, SparseCore 0:
  109.7 130.9 reduce-scatter.1
where the time goes:
time: 248 us
  waiting for transfers between devices  136 us (55%)
  blocking collectives  57.7 us (23%)
  starting transfers between devices  32.7 us (13%)
  between operations  14.2 us (6%)
  local copies, waits for them, and re-layouts  4.31 us (2%)
  other arithmetic  2.77 us (1%)
    reduce_scatter x1, waiting for transfers between devices, body(): lax.psum_scatter(product_sum, 'tm', scatter_dimension=1, tiled=True)  119 us
    all_gather x1, blocking collectives, body(): range_rows = lax.all_gather(range_field, 'tm', axis=1, tiled=True)  57.7 us
    ppermute x6, starting transfers between devices, extended(): lax.ppermute(head, axis, [((i + 1) % count, i) for i in range(ends)])  16.4 us
    ppermute x6, starting transfers between devices, extended(): lax.ppermute(tail, axis, [(i, (i + 1) % count) for i in range(ends)])  16.2 us
    ppermute x6, waiting for transfers between devices, extended(): lax.ppermute(head, axis, [((i + 1) % count, i) for i in range(ends)])  9.81 us
    ppermute x6, waiting for transfers between devices, extended(): lax.ppermute(tail, axis, [(i, (i + 1) % count) for i in range(ends)])  7.18 us
  transfers between devices with their start and end apart: 13, of which 5 were waited for; matrix products, arithmetic and copies ran while one was open for 2% of the time, Pallas kernels for 0%

commit v1 on v0

v1 whole, which is shorter than its diff:
```python
import functools
import math

import jax
import jax.numpy as jnp
from jax import lax
from jax.experimental import pallas as pl
from jax.experimental.pallas import tpu as pltpu
from jax.sharding import PartitionSpec as P

MESH = pl.DeviceIdType.MESH
SEG = 16
OWN = 16
PAD = 3
ROWS = OWN + 2 * PAD
OWN_T = 4
SLICES = OWN_T + 2 * PAD
SHARE = ((0, 5), (5, 4), (9, 4), (13, 3))


def step_weights():
    centre_value = 6.525
    spread_value = 6.475
    root_order = (3, 0, 2, 1)
    return [
        1.0 / (centre_value + spread_value * math.cos(math.pi * (2 * section + 1) / 8.0))
        for section in root_order
    ]


def at_row(row):
    return (row + PAD) * SEG


class Sems:
    def __init__(self):
        self.names = {}

    def __call__(self, *key):
        return self.names.setdefault(key, len(self.names))


def kernel(
    lats, sem_of, cot, its, rng, noise, grad,
    cin, xin, field4, field3, field2, coef, gathered, relay, part, part_in, total, total_in,
    send, recv, local,
):
    weights = step_weights()
    tm = lax.axis_index("tm")
    lat = lax.axis_index("lat")
    z, y = lax.div(tm, 4), lax.rem(tm, 4)
    z_next, z_prev = lax.rem(z + 1, 4), lax.rem(z + 3, 4)
    lat_next, lat_prev = lax.rem(lat + 1, lats), lax.rem(lat + lats - 1, lats)

    def dev(zz, yy, ll=None):
        return (zz * 4 + yy, lat if ll is None else ll)

    barrier = pltpu.get_barrier_semaphore()

    def greet(device):
        pl.semaphore_signal(barrier, inc=1, device_id=device, device_id_type=MESH)

    for other in (1, 2, 3):
        greet(dev(z, lax.rem(y + other, 4)))
    greet(dev(z, y, lat_next))
    greet(dev(z, y, lat_prev))
    greet(dev(z_next, y))
    greet(dev(z_prev, y))

    @pl.when(y == 0)
    def _():
        for plane in (1, 2, 3):
            greet(dev(z_prev, plane))

    @pl.when(y == 3)
    def _():
        for plane in (0, 1, 2):
            greet(dev(z_next, plane))

    loads = [pltpu.make_async_copy(cot.at[t], cin.at[t], local.at[t]) for t in range(OWN_T)]
    for t in (3, 0, 2, 1):
        loads[t].start()
    load_range = pltpu.make_async_copy(rng, gathered.at[y * 4 + z], local.at[4])
    load_range.start()
    load_its = pltpu.make_async_copy(its, xin, local.at[5])
    load_its.start()

    def zero(ref, t, row, rows):
        ref[t + PAD, pl.ds(at_row(row), rows * SEG), :] = jnp.zeros((rows * SEG, 128), jnp.float32)

    @pl.when(lat == 0)
    def _():
        for ref in (field4, field3, field2):
            for t in range(-PAD, OWN_T + PAD):
                zero(ref, t, -PAD, PAD)

    @pl.when(lat == lats - 1)
    def _():
        for ref in (field4, field3, field2):
            for t in range(-PAD, OWN_T + PAD):
                zero(ref, t, OWN, PAD)

    @pl.when(tm == 0)
    def _():
        for ref in (field4, field3, field2):
            for t in range(-PAD, 0):
                zero(ref, t, -PAD, ROWS)

    @pl.when(tm == 15)
    def _():
        for ref in (field4, field3, field2):
            for t in range(OWN_T, OWN_T + PAD):
                zero(ref, t, -PAD, ROWS)

    for t in (3, 0, 2, 1):
        loads[t].wait()
        for group in range(2):
            for j in range(16):
                field4[t + PAD, pl.ds(at_row(group * 8) + j, 8, stride=SEG), :] = cin[
                    t, group * 8 : group * 8 + 8, j * 128 : j * 128 + 128
                ]
    load_range.wait()

    ends = jnp.logical_or(y == 0, y == 3)

    @pl.when(ends)
    def _():
        pl.semaphore_wait(barrier, 8)

    @pl.when(jnp.logical_not(ends))
    def _():
        pl.semaphore_wait(barrier, 9)

    sends = []

    def copy(key, src, dst, device):
        index = sem_of(*key)
        return pltpu.make_async_remote_copy(
            src_ref=src, dst_ref=dst, send_sem=send.at[index], recv_sem=recv.at[index],
            device_id=device, device_id_type=MESH,
        )

    def start(condition, made):
        if condition is None:
            made.start()
        else:
            pl.when(condition)(made.start)
        sends.append((condition, made))

    def arrived(condition, made):
        if condition is None:
            made.wait_recv()
        else:
            pl.when(condition)(made.wait_recv)

    def block(ref, t, row, rows):
        return ref.at[t + PAD, pl.ds(at_row(row), rows * SEG), :]

    has_lat_prev, has_lat_next = lat > 0, lat < lats - 1

    def range_z(way):
        origin = gathered.at[y * 4 + z]
        return copy(("rz", way), origin, origin, dev(z_next if way > 0 else z_prev, y))

    def range_z_second():
        slot = gathered.at[y * 4 + z_prev]
        return copy(("rz2",), slot, slot, dev(z_next, y))

    def range_y(other):
        slots = gathered.at[pl.ds(y * 4, 4)]
        return copy(("ry", other), slots, slots, dev(z, lax.rem(y + other, 4)))

    def range_lat(way):
        if way > 0:
            src, dst = coef.at[pl.ds(at_row(OWN - 2), 2 * SEG)], coef.at[pl.ds(at_row(-2), 2 * SEG)]
        else:
            src, dst = coef.at[pl.ds(at_row(0), 2 * SEG)], coef.at[pl.ds(at_row(OWN), 2 * SEG)]
        return copy(("rl", way), src, dst, dev(z, y, lat_next if way > 0 else lat_prev))

    def lat_halo(way):
        own = pl.ds(PAD, OWN_T)
        if way > 0:
            src, dst = OWN - PAD, -PAD
        else:
            src, dst = 0, OWN
        return copy(
            ("lat", way),
            field4.at[own, pl.ds(at_row(src), PAD * SEG), :],
            field4.at[own, pl.ds(at_row(dst), PAD * SEG), :],
            dev(z, y, lat_next if way > 0 else lat_prev),
        )

    def slices(way, depth):
        return (OWN_T - depth, -depth) if way > 0 else (depth - 1, OWN_T - 1 + depth)

    def beside(way, depth):
        src, dst = slices(way, depth)
        return copy(
            ("t", way, depth), block(field4, src, 0, OWN), block(field4, dst, 0, OWN), dev(z, y + way)
        )

    def across(way):
        return dev(z_next, 0) if way > 0 else dev(z_prev, 3)

    def to_relay(way, depth, plane):
        first, rows = SHARE[plane]
        src, _ = slices(way, depth)
        return copy(
            ("a", way, depth),
            block(field4, src, first, rows),
            relay.at[(way + 1) // 2, depth - 1, pl.ds(0, rows * SEG)],
            dev(z, plane if way > 0 else 3 - plane),
        )

    def to_relay_send(way, depth, plane):
        first, rows = SHARE[plane]
        src, _ = slices(way, depth)
        return pltpu.make_async_remote_copy(
            src_ref=block(field4, src, first, rows),
            dst_ref=relay.at[(way + 1) // 2, depth - 1, pl.ds(0, rows * SEG)],
            send_sem=send.at[sem_of("as", way, depth, plane)],
            recv_sem=recv.at[sem_of("a", way, depth)],
            device_id=dev(z, plane if way > 0 else 3 - plane),
            device_id_type=MESH,
        )

    def from_relay(way, depth, plane):
        first, rows = SHARE[plane]
        src, dst = slices(way, depth)
        source = (
            block(field4, src, first, rows)
            if plane == 3
            else relay.at[(way + 1) // 2, depth - 1, pl.ds(0, rows * SEG)]
        )
        return copy(("b", way, depth, plane), source, block(field4, dst, first, rows), across(way))

    corners = ((1, -2, 2), (1, OWN, 2), (2, -1, 1), (2, OWN, 1))

    def corner(way, number, crossing):
        depth, row, rows = corners[number]
        src, dst = slices(way, depth)
        return copy(
            ("c", way, number),
            block(field4, src, row, rows),
            block(field4, dst, row, rows),
            across(way) if crossing else dev(z, y + way),
        )

    def is_source(way):
        return jnp.logical_and(y == 3, z < 3) if way > 0 else jnp.logical_and(y == 0, z > 0)

    def is_target(way):
        return jnp.logical_and(y == 0, z > 0) if way > 0 else jnp.logical_and(y == 3, z < 3)

    def is_relay(way, plane):
        return (
            jnp.logical_and(y == plane, z < 3) if way > 0 else jnp.logical_and(y == 3 - plane, z > 0)
        )

    def beside_out(way):
        return y < 3 if way > 0 else y > 0

    def beside_in(way):
        return y > 0 if way > 0 else y < 3

    def lat_edge(row):
        return has_lat_prev if row < 0 else has_lat_next

    def send_slices(depth):
        for way in (1, -1):
            for plane in (0, 1, 2):
                start(is_source(way), to_relay_send(way, depth, plane))
            start(is_source(way), from_relay(way, depth, 3))
            start(beside_out(way), beside(way, depth))

    def forward(depth):
        for way in (1, -1):
            for plane in (0, 1, 2):
                arrived(is_relay(way, plane), to_relay(way, depth, plane))
                start(is_relay(way, plane), from_relay(way, depth, plane))

    def wait_slices(depth):
        for way in (1, -1):
            arrived(beside_in(way), beside(way, depth))
            for plane in range(4):
                arrived(is_target(way), from_relay(way, depth, plane))

    def send_corners():
        for way in (1, -1):
            for number in range(4):
                inside = lat_edge(corners[number][1])
                start(jnp.logical_and(beside_out(way), inside), corner(way, number, False))
                start(jnp.logical_and(is_source(way), inside), corner(way, number, True))

    def wait_corners(depth):
        for way in (1, -1):
            for number in range(4):
                if corners[number][0] == depth:
                    inside = lat_edge(corners[number][1])
                    coming = jnp.logical_or(beside_in(way), is_target(way))
                    arrived(jnp.logical_and(coming, inside), corner(way, number, False))

    lane = lax.broadcasted_iota(jnp.int32, (SEG, 128), 1)

    def row_of(src, t, base):
        return src[t, pl.ds(base, SEG), :]

    def stepped(src, t, base, weight):
        cells = row_of(src, t, base)
        around = (
            row_of(src, t, base - SEG)
            + row_of(src, t, base + SEG)
            + row_of(src, t - 1, base)
            + row_of(src, t + 1, base)
        )
        west = pltpu.roll(cells, 1, 1)
        west = jnp.where(lane == 0, pltpu.roll(west, 1, 0), west)
        east = pltpu.roll(cells, 127, 1)
        east = jnp.where(lane == 127, pltpu.roll(east, SEG - 1, 0), east)
        applied = coef[pl.ds(base, SEG), :] * cells - (around + (west + east))
        return cells - weight * applied

    UNROLL = 8

    def step(dst, src, t_first, t_count, t_stride, weight, outer):
        pieces = OWN // UNROLL

        def piece(i, carry):
            t = t_first + PAD + lax.div(i, pieces) * t_stride
            base = pl.multiple_of(at_row(0) + lax.rem(i, pieces) * (UNROLL * SEG), SEG)
            for row in range(UNROLL):
                here = base + row * SEG
                dst[t, pl.ds(here, SEG), :] = stepped(src, t, here, weight)
            return carry

        lax.fori_loop(0, t_count * pieces, piece, 0)

        def beyond(first, rows):
            def one(i, carry):
                t = t_first + PAD + i * t_stride
                for row in range(first, first + rows):
                    dst[t, pl.ds(at_row(row), SEG), :] = stepped(src, t, at_row(row), weight)
                return carry

            lax.fori_loop(0, t_count, one, 0)

        if outer:
            pl.when(has_lat_prev)(lambda: beyond(-outer, outer))
            pl.when(has_lat_next)(lambda: beyond(OWN, outer))

    def products(terms, first):
        def column(j, carry):
            for group in range(2):
                value = None
                for ref, k, t in terms:
                    adj = ref[t + PAD, pl.ds(at_row(group * 8) + j, 8, stride=SEG), :]
                    x = xin[k - 1, t, group * 8 : group * 8 + 8, pl.ds(pl.multiple_of(j * 128, 128), 128)]
                    term = (-weights[k]) * (adj * x)
                    value = term if value is None else value + term
                slot = lax.rem(j, 4) * 4 + lax.div(j, 4)
                rows = slice(group * 8, group * 8 + 8)
                part[slot, rows, :] = value if first else part[slot, rows, :] + value
            return carry

        lax.fori_loop(0, 16, column, 0)

    start(None, range_z(1))
    start(None, range_z(-1))
    start(has_lat_next, lat_halo(1))
    start(has_lat_prev, lat_halo(-1))
    send_slices(1)
    send_slices(2)
    forward(1)
    arrived(has_lat_prev, lat_halo(1))
    arrived(has_lat_next, lat_halo(-1))
    send_corners()
    forward(2)
    send_slices(3)
    arrived(None, range_z(1))
    start(None, range_z_second())
    load_its.wait()
    products([(field4, 3, t) for t in range(OWN_T)], True)
    arrived(None, range_z(-1))
    forward(3)
    arrived(None, range_z_second())
    for other in (1, 2, 3):
        start(None, range_y(other))
    for other in (1, 2, 3):
        arrived(None, range_y(other))
    for j in range(16):
        slot = (j % 4) * 4 + j // 4
        for group in range(2):
            coef[pl.ds(at_row(group * 8) + j, 8, stride=SEG), :] = (
                gathered[slot, group * 8 : group * 8 + 8, :] + 6.0
            )
    start(has_lat_next, range_lat(1))
    start(has_lat_prev, range_lat(-1))
    arrived(has_lat_prev, range_lat(1))
    arrived(has_lat_next, range_lat(-1))

    step(field3, field4, 1, 2, 1, weights[3], 2)
    wait_slices(1)
    wait_corners(1)
    step(field3, field4, 0, 2, 3, weights[3], 2)
    step(field2, field3, 1, 2, 1, weights[2], 1)
    products([(field3, 2, t) for t in range(OWN_T)] + [(field2, 1, 1), (field2, 1, 2)], False)
    wait_slices(2)
    wait_corners(2)
    pl.when(tm > 0)(lambda: step(field3, field4, -1, 1, 1, weights[3], 1))
    pl.when(tm < 15)(lambda: step(field3, field4, OWN_T, 1, 1, weights[3], 1))
    step(field2, field3, 0, 2, 3, weights[2], 1)
    products([(field2, 1, 0), (field2, 1, 3)], False)

    def sum_y(other):
        target = lax.rem(y + other, 4)
        return copy(("sy", other), part.at[pl.ds(target * 4, 4)], part_in.at[other - 1], dev(z, target))

    def sum_z(number):
        which = (lax.rem(z + 2, 4), z_prev, z_next)[number]
        return copy(("sz", number), total.at[which], total_in.at[number], dev(z_prev if number == 1 else z_next, y))

    def finish(t_first, t_count, t_stride):
        pieces = OWN // UNROLL

        def piece(i, carry):
            t = t_first + PAD + lax.div(i, pieces) * t_stride
            base = pl.multiple_of(at_row(0) + lax.rem(i, pieces) * (UNROLL * SEG), SEG)
            for row in range(UNROLL):
                here = base + row * SEG
                last = stepped(field2, t, here, weights[1])
                noise[t - PAD, pl.ds(here - at_row(0), SEG), :] = (
                    weights[3] * row_of(field4, t, here)
                    + weights[2] * row_of(field3, t, here)
                    + weights[1] * row_of(field2, t, here)
                    + weights[0] * last
                )
            return carry

        lax.fori_loop(0, t_count * pieces, piece, 0)

    for other in (1, 2, 3):
        start(None, sum_y(other))
    finish(1, 2, 1)
    for other in (1, 2, 3):
        arrived(None, sum_y(other))
    for zz in range(4):
        total[zz] = part[y * 4 + zz] + part_in[0, zz] + part_in[1, zz] + part_in[2, zz]
    start(None, sum_z(0))
    start(None, sum_z(1))
    wait_slices(3)
    pl.when(tm > 0)(lambda: step(field3, field4, -2, 1, 1, weights[3], 0))
    pl.when(tm < 15)(lambda: step(field3, field4, OWN_T + 1, 1, 1, weights[3], 0))
    pl.when(tm > 0)(lambda: step(field2, field3, -1, 1, 1, weights[2], 0))
    pl.when(tm < 15)(lambda: step(field2, field3, OWN_T, 1, 1, weights[2], 0))
    arrived(None, sum_z(0))
    total[z_next] = total[z_next] + total_in[0]
    start(None, sum_z(2))
    finish(0, 2, 3)
    arrived(None, sum_z(1))
    arrived(None, sum_z(2))
    grad[...] = total[z] + total_in[1] + total_in[2]

    for condition, made in sends:
        if condition is None:
            made.wait_send()
        else:
            pl.when(condition)(made.wait_send)


def place(noise_rows, grad_in, noise, grad):
    def columns(i, carry):
        t, j = lax.div(i, 16), lax.rem(i, 16)
        for group in range(2):
            noise[t, group * 8 : group * 8 + 8, pl.ds(pl.multiple_of(j * 128, 128), 128)] = noise_rows[
                t, pl.ds(group * 8 * SEG + j, 8, stride=SEG), :
            ]
        return carry

    lax.fori_loop(0, OWN_T * 16, columns, 0)
    grad[...] = grad_in[...]


def vmem(*shape):
    return pltpu.VMEM(shape, jnp.float32)


def body(lats, cotangent, iterates, range_field):
    anywhere = pl.BlockSpec(memory_space=pl.ANY)
    inside = pl.BlockSpec(memory_space=pltpu.VMEM)
    count = 128
    noise_rows, grad = pl.pallas_call(
        functools.partial(kernel, lats, Sems()),
        out_shape=(
            jax.ShapeDtypeStruct((OWN_T, OWN * SEG, 128), jnp.float32),
            jax.ShapeDtypeStruct(range_field.shape, jnp.float32),
        ),
        in_specs=[anywhere] * 3,
        out_specs=(inside, inside),
        scratch_shapes=[
            vmem(OWN_T, OWN, 2048),
            vmem(3, OWN_T, OWN, 2048),
            vmem(SLICES, ROWS * SEG, 128),
            vmem(SLICES, ROWS * SEG, 128),
            vmem(SLICES, ROWS * SEG, 128),
            vmem(ROWS * SEG, 128),
            vmem(16, OWN, 128),
            vmem(2, PAD, 5 * SEG, 128),
            vmem(16, OWN, 128),
            vmem(3, 4, OWN, 128),
            vmem(4, OWN, 128),
            vmem(3, OWN, 128),
            pltpu.SemaphoreType.DMA((count,)),
            pltpu.SemaphoreType.DMA((count,)),
            pltpu.SemaphoreType.DMA((6,)),
        ],
        compiler_params=pltpu.CompilerParams(
            collective_id=0, has_side_effects=True, vmem_limit_bytes=32 << 20
        ),
        name="adjoint",
    )(cotangent, iterates, range_field)
    return pl.pallas_call(
        place,
        out_shape=(
            jax.ShapeDtypeStruct(cotangent.shape, jnp.float32),
            jax.ShapeDtypeStruct(range_field.shape, jnp.float32),
        ),
        in_specs=[inside, inside],
        out_specs=(inside, inside),
        name="place",
    )(noise_rows, grad)


def solution(mesh):
    placed = (P("tm", "lat", None), P(None, "tm", "lat", None), P("lat", "tm"))
    return jax.shard_map(
        functools.partial(body, mesh.shape["lat"]),
        mesh=mesh,
        in_specs=placed,
        out_specs=(P("tm", "lat", None), P("lat", "tm")),
        check_vma=False,
    )
```

time: 248 us -> 65.2 us (0.26)
  waiting for transfers between devices: 136 us -> 0 us
  Pallas kernels: 0 us -> 59.8 us
  blocking collectives: 57.7 us -> 0 us
  starting transfers between devices: 32.7 us -> 0 us
  between operations: 14.2 us -> 0.66 us
  other arithmetic: 2.77 us -> 0 us
    reduce_scatter x1 -> x0, waiting for transfers between devices: 119 us -> none  [body(): lax.psum_scatter(product_sum, 'tm', scatter_dimension=1, tiled=True)]
    pallas_call x0 -> x2, Pallas kernels: none -> 59.8 us  [the longest x1 57.2 us: body(): pl.pallas_call(functools.partial(kernel, lats, Sems()), out_shape=(jax.Sh...]
    all_gather x1 -> x0, blocking collectives: 57.7 us -> none  [body(): range_rows = lax.all_gather(range_field, 'tm', axis=1, tiled=True)]
    ppermute x12 -> x0, starting transfers between devices: 32.7 us -> none  [the longest x6 16.4 us: extended(): lax.ppermute(head, axis, [((i + 1) % count, i) for i in range(ends)])]
    ppermute x12 -> x0, waiting for transfers between devices: 17 us -> none  [the longest x6 9.81 us: extended(): lax.ppermute(head, axis, [((i + 1) % count, i) for i in range(ends)])]
    unnamed x6 -> x10, local copies, waits for them, and re-layouts: 0.02 us -> 4.51 us
    slice x12 -> x0, local copies, waits for them, and re-layouts: 4.29 us -> none  [the longest x6 2.04 us: stencil(): longitude = jnp.roll(field, 1, 2) + jnp.roll(field, -1, 2)]
  transfers between devices with their start and end apart: 13 -> 0, of which waited for: 5 -> 0; matrix products, arithmetic and copies ran while one was open for 2% -> 0% of each run, Pallas kernels for 0% -> 0%
where the time goes in v1:
time: 65.2 us; the launch traced here: 65 us
  Pallas kernels  59.8 us (92%)
  local copies, waits for them, and re-layouts  4.51 us (7%)
  between operations  0.66 us (1%)
    pallas_call x1, Pallas kernels, body(): pl.pallas_call(functools.partial(kernel, lats, Sems()), out_shape=(jax.Sh...  57.2 us
    unnamed x10, local copies, waits for them, and re-layouts  4.51 us
    pallas_call x1, Pallas kernels, body(): pl.pallas_call(place, out_shape=(jax.ShapeDtypeStruct(cotangent.shape, jn...  2.57 us

profile of v1, /device:TPU:6, one launch (start us, length us, event | category | flops | bytes accessed | tf_op | source)
XLA Modules:
  0.0 65.0 jit_solution(3873187229577403403)
XLA Ops:
  0.6 0.0 copy-start
  0.6 1.4 %copy-done = f32[3,4,16,2048]{3,2,1,0:T(8,128)S(1)} copy-done((f32[3,4,16,2048]{3,2,1,0:T(8,128)S(1)}, f32[3,4,16,2048]{3,2,1,0:T(8,128)}, u32[]{:S(2)}) %copy-start) | copy-done | bytes 1572888
  2.0 0.0 copy-start.2
  2.0 1.0 %copy-done.2 = f32[4,16,2048]{2,1,0:T(8,128)S(1)} copy-done((f32[4,16,2048]{2,1,0:T(8,128)S(1)}, f32[4,16,2048]{2,1,0:T(8,128)}, u32[]{:S(2)}) %copy-start.2) | copy-done | bytes 524312
  3.1 0.0 copy-start.3
  3.1 0.7 %copy-done.3 = f32[16,128]{1,0:T(8,128)S(1)} copy-done((f32[16,128]{1,0:T(8,128)S(1)}, f32[16,128]{1,0:T(8,128)}, u32[]{:S(2)}) %copy-start.3) | copy-done | bytes 8216
  3.8 57.2 %adjoint.1 = (f32[4,256,128]{2,1,0:T(8,128)S(1)}, f32[16,128]{1,0:T(8,128)S(1)}) custom-call(f32[4,16,2048]{2,1,0:T(8,128)S(1)} %copy-done.2, f32[3,4,16,2048]{3,2,1,0:T(8,128)S(1)} %copy-done, f32[16,128]{1,0:T(8,128)S(1)} %copy-done.3), custom_call_target="tpu_custom_call" | custom-call | tf_op jit(solution)/shard_map/adjoint/pallas_call | solution.py:491
  61.0 0.0 copy-start.1
  61.0 0.8 %copy-done.1 = f32[4,256,128]{2,1,0:T(8,128)} copy-done((f32[4,256,128]{2,1,0:T(8,128)}, f32[4,256,128]{2,1,0:T(8,128)S(1)}, u32[]{:S(2)}) %copy-start.1) | copy-done | bytes 524312
  61.8 0.0 copy-start.4
  61.8 0.6 copy-done.4
  62.4 2.6 %place.1 = (f32[4,16,2048]{2,1,0:T(8,128)}, f32[16,128]{1,0:T(8,128)}) custom-call(f32[4,256,128]{2,1,0:T(8,128)} %copy-done.1, f32[16,128]{1,0:T(8,128)} %copy-done.4), custom_call_target="tpu_custom_call" | custom-call | tf_op jit(solution)/shard_map/place/pallas_call | solution.py:521
Async XLA Ops:
  0.6 1.4 %copy-start = (f32[3,4,16,2048]{3,2,1,0:T(8,128)S(1)}, f32[3,4,16,2048]{3,2,1,0:T(8,128)}, u32[]{:S(2)}) copy-start(f32[3,4,16,2048]{3,2,1,0:T(8,128)} %its.1) | copy-start | bytes 4718596
  2.0 1.0 %copy-start.2 = (f32[4,16,2048]{2,1,0:T(8,128)S(1)}, f32[4,16,2048]{2,1,0:T(8,128)}, u32[]{:S(2)}) copy-start(f32[4,16,2048]{2,1,0:T(8,128)} %cot.1) | copy-start | bytes 1572868
  3.1 0.7 %copy-start.3 = (f32[16,128]{1,0:T(8,128)S(1)}, f32[16,128]{1,0:T(8,128)}, u32[]{:S(2)}) copy-start(f32[16,128]{1,0:T(8,128)} %rng.1) | copy-start | bytes 24580
  61.0 0.8 %copy-start.1 = (f32[4,256,128]{2,1,0:T(8,128)}, f32[4,256,128]{2,1,0:T(8,128)S(1)}, u32[]{:S(2)}) copy-start(f32[4,256,128]{2,1,0:T(8,128)S(1)} %get-tuple-element.4.noise_rows) | copy-start | bytes 1572868
  61.8 0.6 copy-start.4

commit v2 on v1

--- a/solution.py
+++ b/solution.py
@@ -42,7 +42,7 @@
 
 def kernel(
     lats, sem_of, cot, its, rng, noise, grad,
-    cin, xin, field4, field3, field2, coef, gathered, relay, part, part_in, total, total_in,
+    cin, xin, field4, field3, field2, rows_out, coef, gathered, relay, part, part_in, total, total_in,
     send, recv, local,
 ):
     weights = step_weights()
@@ -60,22 +60,23 @@
     def greet(device):
         pl.semaphore_signal(barrier, inc=1, device_id=device, device_id_type=MESH)
 
+    greet(dev(z_next, y))
+    greet(dev(z_prev, y))
+
+    @pl.when(y == 0)
+    def _():
+        for plane in (1, 2, 3):
+            greet(dev(z_prev, plane))
+
+    @pl.when(y == 3)
+    def _():
+        for plane in (0, 1, 2):
+            greet(dev(z_next, plane))
+
+    greet(dev(z, y, lat_next))
+    greet(dev(z, y, lat_prev))
     for other in (1, 2, 3):
         greet(dev(z, lax.rem(y + other, 4)))
-    greet(dev(z, y, lat_next))
-    greet(dev(z, y, lat_prev))
-    greet(dev(z_next, y))
-    greet(dev(z_prev, y))
-
-    @pl.when(y == 0)
-    def _():
-        for plane in (1, 2, 3):
-            greet(dev(z_prev, plane))
-
-    @pl.when(y == 3)
-    def _():
-        for plane in (0, 1, 2):
-            greet(dev(z_next, plane))
 
     loads = [pltpu.make_async_copy(cot.at[t], cin.at[t], local.at[t]) for t in range(OWN_T)]
     for t in (3, 0, 2, 1):
@@ -140,18 +141,43 @@
             device_id=device, device_id_type=MESH,
         )
 
-    def start(condition, made):
+    def start(condition, *made):
         if condition is None:
-            made.start()
+            for one in made:
+                one.start()
         else:
-            pl.when(condition)(made.start)
+
+            @pl.when(condition)
+            def _():
+                for one in made:
+                    one.start()
+
         sends.append((condition, made))
 
-    def arrived(condition, made):
+    def arrived(condition, *made):
         if condition is None:
-            made.wait_recv()
+            for one in made:
+                one.wait_recv()
         else:
-            pl.when(condition)(made.wait_recv)
+
+            @pl.when(condition)
+            def _():
+                for one in made:
+                    one.wait_recv()
+
+    def sent():
+        for condition, made in sends:
+            if condition is None:
+                for one in made:
+                    one.wait_send()
+            else:
+
+                @pl.when(condition)
+                def _():
+                    for one in made:
+                        one.wait_send()
+
+        sends.clear()
 
     def block(ref, t, row, rows):
         return ref.at[t + PAD, pl.ds(at_row(row), rows * SEG), :]
@@ -166,9 +192,13 @@
         slot = gathered.at[y * 4 + z_prev]
         return copy(("rz2",), slot, slot, dev(z_next, y))
 
-    def range_y(other):
-        slots = gathered.at[pl.ds(y * 4, 4)]
-        return copy(("ry", other), slots, slots, dev(z, lax.rem(y + other, 4)))
+    def range_y(number, other):
+        slot = gathered.at[y * 4 + (z, z_prev, z_next, lax.rem(z + 2, 4))[number]]
+        return copy(("ry", number, other), slot, slot, dev(z, lax.rem(y + other, 4)))
+
+    def share_range(number):
+        for other in (1, 2, 3):
+            start(None, range_y(number, other))
 
     def range_lat(way):
         if way > 0:
@@ -268,29 +298,41 @@
 
     def send_slices(depth):
         for way in (1, -1):
-            for plane in (0, 1, 2):
-                start(is_source(way), to_relay_send(way, depth, plane))
-            start(is_source(way), from_relay(way, depth, 3))
+            start(
+                is_source(way),
+                *[to_relay_send(way, depth, plane) for plane in (0, 1, 2)],
+                from_relay(way, depth, 3),
+            )
             start(beside_out(way), beside(way, depth))
 
     def forward(depth):
         for way in (1, -1):
             for plane in (0, 1, 2):
-                arrived(is_relay(way, plane), to_relay(way, depth, plane))
-                start(is_relay(way, plane), from_relay(way, depth, plane))
+
+                @pl.when(is_relay(way, plane))
+                def _():
+                    to_relay(way, depth, plane).wait_recv()
+                    from_relay(way, depth, plane).start()
+
+                sends.append((is_relay(way, plane), (from_relay(way, depth, plane),)))
 
     def wait_slices(depth):
         for way in (1, -1):
             arrived(beside_in(way), beside(way, depth))
-            for plane in range(4):
-                arrived(is_target(way), from_relay(way, depth, plane))
+            arrived(is_target(way), *[from_relay(way, depth, plane) for plane in range(4)])
 
     def send_corners():
         for way in (1, -1):
-            for number in range(4):
-                inside = lat_edge(corners[number][1])
-                start(jnp.logical_and(beside_out(way), inside), corner(way, number, False))
-                start(jnp.logical_and(is_source(way), inside), corner(way, number, True))
+            for pair in ((0, 2), (1, 3)):
+                inside = lat_edge(corners[pair[0]][1])
+                start(
+                    jnp.logical_and(beside_out(way), inside),
+                    *[corner(way, number, False) for number in pair],
+                )
+                start(
+                    jnp.logical_and(is_source(way), inside),
+                    *[corner(way, number, True) for number in pair],
+                )
 
     def wait_corners(depth):
         for way in (1, -1):
@@ -305,7 +347,7 @@
     def row_of(src, t, base):
         return src[t, pl.ds(base, SEG), :]
 
-    def stepped(src, t, base, weight):
+    def neighbours(src, t, base):
         cells = row_of(src, t, base)
         around = (
             row_of(src, t, base - SEG)
@@ -317,12 +359,25 @@
         west = jnp.where(lane == 0, pltpu.roll(west, 1, 0), west)
         east = pltpu.roll(cells, 127, 1)
         east = jnp.where(lane == 127, pltpu.roll(east, SEG - 1, 0), east)
-        applied = coef[pl.ds(base, SEG), :] * cells - (around + (west + east))
-        return cells - weight * applied
+        return around + (west + east)
+
+    def joined(src, t, base, weight, summed):
+        cells = row_of(src, t, base)
+        return cells - weight * (coef[pl.ds(base, SEG), :] * cells - summed)
+
+    def stepped(src, t, base, weight):
+        return joined(src, t, base, weight, neighbours(src, t, base))
 
     UNROLL = 8
 
-    def step(dst, src, t_first, t_count, t_stride, weight, outer):
+    def step(dst, src, t_first, t_count, t_stride, weight, outer, how=None):
+        def stepped_by(src, t, base, weight):
+            if how == "gather":
+                return neighbours(src, t, base)
+            if how == "join":
+                return joined(src, t, base, weight, row_of(dst, t, base))
+            return stepped(src, t, base, weight)
+
         pieces = OWN // UNROLL
 
         def piece(i, carry):
@@ -330,7 +385,7 @@
             base = pl.multiple_of(at_row(0) + lax.rem(i, pieces) * (UNROLL * SEG), SEG)
             for row in range(UNROLL):
                 here = base + row * SEG
-                dst[t, pl.ds(here, SEG), :] = stepped(src, t, here, weight)
+                dst[t, pl.ds(here, SEG), :] = stepped_by(src, t, here, weight)
             return carry
 
         lax.fori_loop(0, t_count * pieces, piece, 0)
@@ -339,7 +394,7 @@
             def one(i, carry):
                 t = t_first + PAD + i * t_stride
                 for row in range(first, first + rows):
-                    dst[t, pl.ds(at_row(row), SEG), :] = stepped(src, t, at_row(row), weight)
+                    dst[t, pl.ds(at_row(row), SEG), :] = stepped_by(src, t, at_row(row), weight)
                 return carry
 
             lax.fori_loop(0, t_count, one, 0)
@@ -368,25 +423,28 @@
     start(None, range_z(-1))
     start(has_lat_next, lat_halo(1))
     start(has_lat_prev, lat_halo(-1))
+    share_range(0)
     send_slices(1)
+    forward(1)
+    arrived(None, range_z(1))
+    start(None, range_z_second())
+    share_range(1)
+    arrived(None, range_z(-1))
+    share_range(2)
     send_slices(2)
-    forward(1)
     arrived(has_lat_prev, lat_halo(1))
     arrived(has_lat_next, lat_halo(-1))
     send_corners()
     forward(2)
-    send_slices(3)
-    arrived(None, range_z(1))
-    start(None, range_z_second())
     load_its.wait()
     products([(field4, 3, t) for t in range(OWN_T)], True)
-    arrived(None, range_z(-1))
-    forward(3)
     arrived(None, range_z_second())
-    for other in (1, 2, 3):
-        start(None, range_y(other))
-    for other in (1, 2, 3):
-        arrived(None, range_y(other))
+    share_range(3)
+    send_slices(3)
+    step(field3, field4, 1, 2, 1, weights[3], 2, "gather")
+    for number in range(4):
+        for other in (1, 2, 3):
+            arrived(None, range_y(number, other))
     for j in range(16):
         slot = (j % 4) * 4 + j // 4
         for group in range(2):
@@ -395,13 +453,13 @@
             )
     start(has_lat_next, range_lat(1))
     start(has_lat_prev, range_lat(-1))
+    wait_slices(1)
+    wait_corners(1)
+    step(field3, field4, 0, 2, 3, weights[3], 2, "gather")
+    forward(3)
     arrived(has_lat_prev, range_lat(1))
     arrived(has_lat_next, range_lat(-1))
-
-    step(field3, field4, 1, 2, 1, weights[3], 2)
-    wait_slices(1)
-    wait_corners(1)
-    step(field3, field4, 0, 2, 3, weights[3], 2)
+    step(field3, field4, 0, 4, 1, weights[3], 2, "join")
     step(field2, field3, 1, 2, 1, weights[2], 1)
     products([(field3, 2, t) for t in range(OWN_T)] + [(field2, 1, 1), (field2, 1, 2)], False)
     wait_slices(2)
@@ -428,7 +486,7 @@
             for row in range(UNROLL):
                 here = base + row * SEG
                 last = stepped(field2, t, here, weights[1])
-                noise[t - PAD, pl.ds(here - at_row(0), SEG), :] = (
+                rows_out[t - PAD, pl.ds(here - at_row(0), SEG), :] = (
                     weights[3] * row_of(field4, t, here)
                     + weights[2] * row_of(field3, t, here)
                     + weights[1] * row_of(field2, t, here)
@@ -437,6 +495,17 @@
             return carry
 
         lax.fori_loop(0, t_count * pieces, piece, 0)
+
+        def columns(i, carry):
+            t = t_first + lax.div(i, 16) * t_stride
+            j = lax.rem(i, 16)
+            for group in range(2):
+                noise[t, group * 8 : group * 8 + 8, pl.ds(pl.multiple_of(j * 128, 128), 128)] = rows_out[
+                    t, pl.ds(group * 8 * SEG + j, 8, stride=SEG), :
+                ]
+            return carry
+
+        lax.fori_loop(0, t_count * 16, columns, 0)
 
     for other in (1, 2, 3):
         start(None, sum_y(other))
@@ -445,8 +514,7 @@
         arrived(None, sum_y(other))
     for zz in range(4):
         total[zz] = part[y * 4 + zz] + part_in[0, zz] + part_in[1, zz] + part_in[2, zz]
-    start(None, sum_z(0))
-    start(None, sum_z(1))
+    start(None, sum_z(0), sum_z(1))
     wait_slices(3)
     pl.when(tm > 0)(lambda: step(field3, field4, -2, 1, 1, weights[3], 0))
     pl.when(tm < 15)(lambda: step(field3, field4, OWN_T + 1, 1, 1, weights[3], 0))
@@ -456,28 +524,21 @@
     total[z_next] = total[z_next] + total_in[0]
     start(None, sum_z(2))
     finish(0, 2, 3)
+    sent()
     arrived(None, sum_z(1))
     arrived(None, sum_z(2))
     grad[...] = total[z] + total_in[1] + total_in[2]
 
-    for condition, made in sends:
-        if condition is None:
-            made.wait_send()
-        else:
-            pl.when(condition)(made.wait_send)
-
-
-def place(noise_rows, grad_in, noise, grad):
-    def columns(i, carry):
-        t, j = lax.div(i, 16), lax.rem(i, 16)
-        for group in range(2):
-            noise[t, group * 8 : group * 8 + 8, pl.ds(pl.multiple_of(j * 128, 128), 128)] = noise_rows[
-                t, pl.ds(group * 8 * SEG + j, 8, stride=SEG), :
-            ]
-        return carry
-
-    lax.fori_loop(0, OWN_T * 16, columns, 0)
-    grad[...] = grad_in[...]
+
+def place(noise_in, grad_in, noise, grad, done):
+    copies = [
+        pltpu.make_async_copy(noise_in, noise, done.at[0]),
+        pltpu.make_async_copy(grad_in, grad, done.at[1]),
+    ]
+    for one in copies:
+        one.start()
+    for one in copies:
+        one.wait()
 
 
 def vmem(*shape):
@@ -485,13 +546,13 @@
 
 
 def body(lats, cotangent, iterates, range_field):
-    anywhere = pl.BlockSpec(memory_space=pl.ANY)
+    anywhere = pl.BlockSpec(memory_space=pltpu.HBM)
     inside = pl.BlockSpec(memory_space=pltpu.VMEM)
     count = 128
-    noise_rows, grad = pl.pallas_call(
+    return pl.pallas_call(
         functools.partial(kernel, lats, Sems()),
         out_shape=(
-            jax.ShapeDtypeStruct((OWN_T, OWN * SEG, 128), jnp.float32),
+            jax.ShapeDtypeStruct(cotangent.shape, jnp.float32),
             jax.ShapeDtypeStruct(range_field.shape, jnp.float32),
         ),
         in_specs=[anywhere] * 3,
@@ -502,6 +563,7 @@
             vmem(SLICES, ROWS * SEG, 128),
             vmem(SLICES, ROWS * SEG, 128),
             vmem(SLICES, ROWS * SEG, 128),
+            vmem(OWN_T, OWN * SEG, 128),
             vmem(ROWS * SEG, 128),
             vmem(16, OWN, 128),
             vmem(2, PAD, 5 * SEG, 128),
@@ -514,20 +576,10 @@
             pltpu.SemaphoreType.DMA((6,)),
         ],
         compiler_params=pltpu.CompilerParams(
-            collective_id=0, has_side_effects=True, vmem_limit_bytes=32 << 20
+            collective_id=0, has_side_effects=True, vmem_limit_bytes=60 << 20
         ),
         name="adjoint",
     )(cotangent, iterates, range_field)
-    return pl.pallas_call(
-        place,
-        out_shape=(
-            jax.ShapeDtypeStruct(cotangent.shape, jnp.float32),
-            jax.ShapeDtypeStruct(range_field.shape, jnp.float32),
-        ),
-        in_specs=[inside, inside],
-        out_specs=(inside, inside),
-        name="place",
-    )(noise_rows, grad)
 
 
 def solution(mesh):

time: 65.2 us -> 56.2 us (0.86)
  Pallas kernels: 59.8 us -> 51.5 us
  local copies, waits for them, and re-layouts: 4.51 us -> 3.17 us
    pallas_call x1, Pallas kernels: 57.2 us -> 51.5 us  [body(): pl.pallas_call(functools.partial(kernel, lats, Sems()), out_shape=(jax.Sh...]
    pallas_call x1 -> x0, Pallas kernels: 2.57 us -> none  [body(): pl.pallas_call(place, out_shape=(jax.ShapeDtypeStruct(cotangent.shape, jn...]
    unnamed x10 -> x2, local copies, waits for them, and re-layouts: 4.51 us -> 3.17 us
where the time goes in v2:
time: 56.2 us; the launch traced here: 55.3 us
  Pallas kernels  51.5 us (92%)
  local copies, waits for them, and re-layouts  3.17 us (6%)
  between operations  0.64 us (1%)
    pallas_call x1, Pallas kernels, body(): pl.pallas_call(functools.partial(kernel, lats, Sems()), out_shape=(jax.Sh...  51.5 us
    unnamed x2, local copies, waits for them, and re-layouts  3.17 us

profile of v2, /device:TPU:6, one launch (start us, length us, event | category | flops | bytes accessed | tf_op | source)
XLA Modules:
  0.0 55.3 jit_solution(9625732833478127344)
XLA Ops:
  0.6 51.5 %adjoint.1 = (f32[4,16,2048]{2,1,0:T(8,128)}, f32[16,128]{1,0:T(8,128)}) custom-call(f32[4,16,2048]{2,1,0:T(8,128)} %cot.1, f32[3,4,16,2048]{3,2,1,0:T(8,128)} %its.1, f32[16,128]{1,0:T(8,128)} %rng.1), custom_call_target="tpu_custom_call" | custom-call | tf_op jit(solution)/shard_map/adjoint/pallas_call | solution.py:552
  52.2 1.9 %copy.7 = f32[4,16,2048]{2,1,0:T(8,128)} copy(f32[4,16,2048]{2,1,0:T(8,128)} %get-tuple-element.4) | data formatting | bytes 1048576
  54.0 1.3 %copy.8 = f32[16,128]{1,0:T(8,128)} copy(f32[16,128]{1,0:T(8,128)} %get-tuple-element.5) | data formatting | bytes 16384

commit v3 on v2

--- a/solution.py
+++ b/solution.py
@@ -42,14 +42,14 @@
 
 def kernel(
     lats, sem_of, cot, its, rng, noise, grad,
-    cin, xin, field4, field3, field2, rows_out, coef, gathered, relay, part, part_in, total, total_in,
+    cin, xin, field4, field3, field2, rows_out, coef, gathered, edges, relay, part, part_in, total, total_in,
     send, recv, local,
 ):
     weights = step_weights()
     tm = lax.axis_index("tm")
     lat = lax.axis_index("lat")
     z, y = lax.div(tm, 4), lax.rem(tm, 4)
-    z_next, z_prev = lax.rem(z + 1, 4), lax.rem(z + 3, 4)
+    z_next, z_prev, z_far = lax.rem(z + 1, 4), lax.rem(z + 3, 4), lax.rem(z + 2, 4)
     lat_next, lat_prev = lax.rem(lat + 1, lats), lax.rem(lat + lats - 1, lats)
 
     def dev(zz, yy, ll=None):
@@ -60,8 +60,8 @@
     def greet(device):
         pl.semaphore_signal(barrier, inc=1, device_id=device, device_id_type=MESH)
 
-    greet(dev(z_next, y))
-    greet(dev(z_prev, y))
+    for other in (z_next, z_prev):
+        greet(dev(other, y))
 
     @pl.when(y == 0)
     def _():
@@ -73,10 +73,11 @@
         for plane in (0, 1, 2):
             greet(dev(z_next, plane))
 
-    greet(dev(z, y, lat_next))
-    greet(dev(z, y, lat_prev))
-    for other in (1, 2, 3):
-        greet(dev(z, lax.rem(y + other, 4)))
+    for other in range(4):
+        greet(dev(z, lax.rem(y + other, 4), lat_next))
+        greet(dev(z, lax.rem(y + other, 4), lat_prev))
+        if other:
+            greet(dev(z, lax.rem(y + other, 4)))
 
     loads = [pltpu.make_async_copy(cot.at[t], cin.at[t], local.at[t]) for t in range(OWN_T)]
     for t in (3, 0, 2, 1):
@@ -113,24 +114,15 @@
             for t in range(OWN_T, OWN_T + PAD):
                 zero(ref, t, -PAD, ROWS)
 
-    for t in (3, 0, 2, 1):
-        loads[t].wait()
-        for group in range(2):
-            for j in range(16):
-                field4[t + PAD, pl.ds(at_row(group * 8) + j, 8, stride=SEG), :] = cin[
-                    t, group * 8 : group * 8 + 8, j * 128 : j * 128 + 128
-                ]
-    load_range.wait()
-
     ends = jnp.logical_or(y == 0, y == 3)
 
     @pl.when(ends)
     def _():
-        pl.semaphore_wait(barrier, 8)
+        pl.semaphore_wait(barrier, 14)
 
     @pl.when(jnp.logical_not(ends))
     def _():
-        pl.semaphore_wait(barrier, 9)
+        pl.semaphore_wait(barrier, 15)
 
     sends = []
 
@@ -185,27 +177,28 @@
     has_lat_prev, has_lat_next = lat > 0, lat < lats - 1
 
     def range_z(way):
-        origin = gathered.at[y * 4 + z]
-        return copy(("rz", way), origin, origin, dev(z_next if way > 0 else z_prev, y))
+        return copy(("rz", way), rng, gathered.at[y * 4 + z], dev(z_next if way > 0 else z_prev, y))
 
     def range_z_second():
         slot = gathered.at[y * 4 + z_prev]
         return copy(("rz2",), slot, slot, dev(z_next, y))
 
     def range_y(number, other):
-        slot = gathered.at[y * 4 + (z, z_prev, z_next, lax.rem(z + 2, 4))[number]]
+        slot = gathered.at[y * 4 + (z, z_prev, z_next, z_far)[number]]
         return copy(("ry", number, other), slot, slot, dev(z, lax.rem(y + other, 4)))
 
     def share_range(number):
         for other in (1, 2, 3):
             start(None, range_y(number, other))
 
-    def range_lat(way):
-        if way > 0:
-            src, dst = coef.at[pl.ds(at_row(OWN - 2), 2 * SEG)], coef.at[pl.ds(at_row(-2), 2 * SEG)]
-        else:
-            src, dst = coef.at[pl.ds(at_row(0), 2 * SEG)], coef.at[pl.ds(at_row(OWN), 2 * SEG)]
-        return copy(("rl", way), src, dst, dev(z, y, lat_next if way > 0 else lat_prev))
+    def range_edge(way, other):
+        slots = pl.ds(y * 4, 4)
+        return copy(
+            ("re", way, other),
+            gathered.at[slots, pl.ds(8 if way > 0 else 0, 8), :],
+            edges.at[0 if way > 0 else 1, slots],
+            dev(z, lax.rem(y + other, 4), lat_next if way > 0 else lat_prev),
+        )
 
     def lat_halo(way):
         own = pl.ds(PAD, OWN_T)
@@ -419,27 +412,37 @@
 
         lax.fori_loop(0, 16, column, 0)
 
-    start(None, range_z(1))
-    start(None, range_z(-1))
+    start(None, range_z(1), range_z(-1))
+    load_range.wait()
+    share_range(0)
+
+    for t in (3, 0, 2, 1):
+        loads[t].wait()
+        for group in range(2):
+            for j in range(16):
+                field4[t + PAD, pl.ds(at_row(group * 8) + j, 8, stride=SEG), :] = cin[
+                    t, group * 8 : group * 8 + 8, j * 128 : j * 128 + 128
+                ]
     start(has_lat_next, lat_halo(1))
     start(has_lat_prev, lat_halo(-1))
-    share_range(0)
     send_slices(1)
-    forward(1)
     arrived(None, range_z(1))
     start(None, range_z_second())
     share_range(1)
     arrived(None, range_z(-1))
     share_range(2)
+    forward(1)
+    arrived(None, range_z_second())
+    share_range(3)
+    start(has_lat_next, *[range_edge(1, other) for other in range(4)])
+    start(has_lat_prev, *[range_edge(-1, other) for other in range(4)])
     send_slices(2)
     arrived(has_lat_prev, lat_halo(1))
     arrived(has_lat_next, lat_halo(-1))
     send_corners()
-    forward(2)
     load_its.wait()
     products([(field4, 3, t) for t in range(OWN_T)], True)
-    arrived(None, range_z_second())
-    share_range(3)
+    forward(2)
     send_slices(3)
     step(field3, field4, 1, 2, 1, weights[3], 2, "gather")
     for number in range(4):
@@ -451,14 +454,21 @@
             coef[pl.ds(at_row(group * 8) + j, 8, stride=SEG), :] = (
                 gathered[slot, group * 8 : group * 8 + 8, :] + 6.0
             )
-    start(has_lat_next, range_lat(1))
-    start(has_lat_prev, range_lat(-1))
     wait_slices(1)
     wait_corners(1)
     step(field3, field4, 0, 2, 3, weights[3], 2, "gather")
     forward(3)
-    arrived(has_lat_prev, range_lat(1))
-    arrived(has_lat_next, range_lat(-1))
+
+    def edge_rows(side, row, first):
+        for j in range(16):
+            slot = (j % 4) * 4 + j // 4
+            for i in range(2):
+                coef[pl.ds(at_row(row + i) + j, 1), :] = edges[side, slot, first + i : first + i + 1, :] + 6.0
+
+    arrived(has_lat_prev, *[range_edge(1, other) for other in range(4)])
+    arrived(has_lat_next, *[range_edge(-1, other) for other in range(4)])
+    pl.when(has_lat_prev)(lambda: edge_rows(0, -2, 6))
+    pl.when(has_lat_next)(lambda: edge_rows(1, OWN, 0))
     step(field3, field4, 0, 4, 1, weights[3], 2, "join")
     step(field2, field3, 1, 2, 1, weights[2], 1)
     products([(field3, 2, t) for t in range(OWN_T)] + [(field2, 1, 1), (field2, 1, 2)], False)
@@ -474,8 +484,8 @@
         return copy(("sy", other), part.at[pl.ds(target * 4, 4)], part_in.at[other - 1], dev(z, target))
 
     def sum_z(number):
-        which = (lax.rem(z + 2, 4), z_prev, z_next)[number]
-        return copy(("sz", number), total.at[which], total_in.at[number], dev(z_prev if number == 1 else z_next, y))
+        which = (z_far, z_prev, z_next)[number]
+        return copy(("sz", number), total.at[which], total_in.at[number], dev(which, y))
 
     def finish(t_first, t_count, t_stride):
         pieces = OWN // UNROLL
@@ -514,31 +524,17 @@
         arrived(None, sum_y(other))
     for zz in range(4):
         total[zz] = part[y * 4 + zz] + part_in[0, zz] + part_in[1, zz] + part_in[2, zz]
-    start(None, sum_z(0), sum_z(1))
+    start(None, sum_z(0), sum_z(1), sum_z(2))
     wait_slices(3)
     pl.when(tm > 0)(lambda: step(field3, field4, -2, 1, 1, weights[3], 0))
     pl.when(tm < 15)(lambda: step(field3, field4, OWN_T + 1, 1, 1, weights[3], 0))
     pl.when(tm > 0)(lambda: step(field2, field3, -1, 1, 1, weights[2], 0))
     pl.when(tm < 15)(lambda: step(field2, field3, OWN_T, 1, 1, weights[2], 0))
-    arrived(None, sum_z(0))
-    total[z_next] = total[z_next] + total_in[0]
-    start(None, sum_z(2))
     finish(0, 2, 3)
     sent()
-    arrived(None, sum_z(1))
-    arrived(None, sum_z(2))
-    grad[...] = total[z] + total_in[1] + total_in[2]
-
-
-def place(noise_in, grad_in, noise, grad, done):
-    copies = [
-        pltpu.make_async_copy(noise_in, noise, done.at[0]),
-        pltpu.make_async_copy(grad_in, grad, done.at[1]),
-    ]
-    for one in copies:
-        one.start()
-    for one in copies:
-        one.wait()
+    for number in range(3):
+        arrived(None, sum_z(number))
+    grad[...] = total[z] + total_in[0] + total_in[1] + total_in[2]
 
 
 def vmem(*shape):
@@ -552,8 +548,8 @@
     return pl.pallas_call(
         functools.partial(kernel, lats, Sems()),
         out_shape=(
-            jax.ShapeDtypeStruct(cotangent.shape, jnp.float32),
-            jax.ShapeDtypeStruct(range_field.shape, jnp.float32),
+            vmem(*cotangent.shape),
+            vmem(*range_field.shape),
         ),
         in_specs=[anywhere] * 3,
         out_specs=(inside, inside),
@@ -566,6 +562,7 @@
             vmem(OWN_T, OWN * SEG, 128),
             vmem(ROWS * SEG, 128),
             vmem(16, OWN, 128),
+            vmem(2, 16, 8, 128),
             vmem(2, PAD, 5 * SEG, 128),
             vmem(16, OWN, 128),
             vmem(3, 4, OWN, 128),
@@ -576,7 +573,7 @@
             pltpu.SemaphoreType.DMA((6,)),
         ],
         compiler_params=pltpu.CompilerParams(
-            collective_id=0, has_side_effects=True, vmem_limit_bytes=60 << 20
+            collective_id=0, has_side_effects=True, vmem_limit_bytes=56 << 20
         ),
         name="adjoint",
     )(cotangent, iterates, range_field)

time: 56.2 us -> 54.4 us (0.968); the launches traced: 55.3 us -> 54.2 us
  local copies, waits for them, and re-layouts: 3.17 us -> 1.39 us
  Pallas kernels: 51.5 us -> 52.2 us
    unnamed x2, local copies, waits for them, and re-layouts: 3.17 us -> 1.39 us
    pallas_call x1, Pallas kernels: 51.5 us -> 52.2 us  [body(): pl.pallas_call(functools.partial(kernel, lats, Sems()), out_shape=(vmem(*...]
where the time goes in v3:
time: 54.4 us; the launch traced here: 54.2 us
  Pallas kernels  52.2 us (96%)
  local copies, waits for them, and re-layouts  1.39 us (3%)
  between operations  0.64 us (1%)
    pallas_call x1, Pallas kernels, body(): pl.pallas_call(functools.partial(kernel, lats, Sems()), out_shape=(vmem(*...  52.2 us
    unnamed x2, local copies, waits for them, and re-layouts  1.39 us

profile of v3, /device:TPU:6, one launch (start us, length us, event | category | flops | bytes accessed | tf_op | source)
XLA Modules:
  0.0 54.2 jit_solution(5242551493854758648)
XLA Ops:
  0.6 52.2 %adjoint.1 = (f32[4,16,2048]{2,1,0:T(8,128)S(1)}, f32[16,128]{1,0:T(8,128)S(1)}) custom-call(f32[4,16,2048]{2,1,0:T(8,128)} %cot.1, f32[3,4,16,2048]{3,2,1,0:T(8,128)} %its.1, f32[16,128]{1,0:T(8,128)} %rng.1), custom_call_target="tpu_custom_call" | custom-call | tf_op jit(solution)/shard_map/adjoint/pallas_call | solution.py:548
  52.8 0.8 %copy.7 = f32[4,16,2048]{2,1,0:T(8,128)} copy(f32[4,16,2048]{2,1,0:T(8,128)S(1)} %get-tuple-element.2) | data formatting | bytes 1048576
  53.6 0.6 %copy.8 = f32[16,128]{1,0:T(8,128)} copy(f32[16,128]{1,0:T(8,128)S(1)} %get-tuple-element.3) | data formatting | bytes 16384

commit v4 on v3

--- a/solution.py
+++ b/solution.py
@@ -42,7 +42,7 @@
 
 def kernel(
     lats, sem_of, cot, its, rng, noise, grad,
-    cin, xin, field4, field3, field2, rows_out, coef, gathered, edges, relay, part, part_in, total, total_in,
+    cin, xin, field4, field3, field2, rows_out, xrows, summed, coef, gathered, edges, relay, part, part_in, total, total_in,
     send, recv, local,
 ):
     weights = step_weights()
@@ -363,7 +363,7 @@
 
     UNROLL = 8
 
-    def step(dst, src, t_first, t_count, t_stride, weight, outer, how=None):
+    def step(dst, src, t_first, t_count, t_stride, weight, outer, how=None, k=None):
         def stepped_by(src, t, base, weight):
             if how == "gather":
                 return neighbours(src, t, base)
@@ -378,7 +378,10 @@
             base = pl.multiple_of(at_row(0) + lax.rem(i, pieces) * (UNROLL * SEG), SEG)
             for row in range(UNROLL):
                 here = base + row * SEG
-                dst[t, pl.ds(here, SEG), :] = stepped_by(src, t, here, weight)
+                value = stepped_by(src, t, here, weight)
+                dst[t, pl.ds(here, SEG), :] = value
+                if k is not None:
+                    add_product(k, t - PAD, here - at_row(0), value)
             return carry
 
         lax.fori_loop(0, t_count * pieces, piece, 0)
@@ -396,21 +399,41 @@
             pl.when(has_lat_prev)(lambda: beyond(-outer, outer))
             pl.when(has_lat_next)(lambda: beyond(OWN, outer))
 
-    def products(terms, first):
-        def column(j, carry):
+    def add_product(k, t, row, value):
+        rows = pl.ds(row, SEG)
+        summed[rows, :] = summed[rows, :] - weights[k] * (value * xrows[(k - 1) * OWN_T + t, rows, :])
+
+    def rows_of_x():
+        def column(i, carry):
+            k, j = lax.div(i, 16), lax.rem(i, 16)
+            for t in range(OWN_T):
+                for group in range(2):
+                    xrows[k * OWN_T + t, pl.ds(group * 8 * SEG + j, 8, stride=SEG), :] = xin[
+                        k, t, group * 8 : group * 8 + 8, pl.ds(pl.multiple_of(j * 128, 128), 128)
+                    ]
+            return carry
+
+        lax.fori_loop(0, 48, column, 0)
+
+    def first_products():
+        def piece(i, carry):
+            for row in range(UNROLL):
+                here = pl.multiple_of((i * UNROLL + row) * SEG, SEG)
+                value = None
+                for t in range(OWN_T):
+                    term = row_of(field4, t + PAD, here + at_row(0)) * xrows[2 * OWN_T + t, pl.ds(here, SEG), :]
+                    value = term if value is None else value + term
+                summed[pl.ds(here, SEG), :] = (-weights[3]) * value
+            return carry
+
+        lax.fori_loop(0, OWN // UNROLL, piece, 0)
+
+    def products_out():
+        for j in range(16):
             for group in range(2):
-                value = None
-                for ref, k, t in terms:
-                    adj = ref[t + PAD, pl.ds(at_row(group * 8) + j, 8, stride=SEG), :]
-                    x = xin[k - 1, t, group * 8 : group * 8 + 8, pl.ds(pl.multiple_of(j * 128, 128), 128)]
-                    term = (-weights[k]) * (adj * x)
-                    value = term if value is None else value + term
-                slot = lax.rem(j, 4) * 4 + lax.div(j, 4)
-                rows = slice(group * 8, group * 8 + 8)
-                part[slot, rows, :] = value if first else part[slot, rows, :] + value
-            return carry
-
-        lax.fori_loop(0, 16, column, 0)
+                part[(j % 4) * 4 + j // 4, group * 8 : group * 8 + 8, :] = summed[
+                    pl.ds(group * 8 * SEG + j, 8, stride=SEG), :
+                ]
 
     start(None, range_z(1), range_z(-1))
     load_range.wait()
@@ -426,6 +449,7 @@
     start(has_lat_next, lat_halo(1))
     start(has_lat_prev, lat_halo(-1))
     send_slices(1)
+    send_slices(2)
     arrived(None, range_z(1))
     start(None, range_z_second())
     share_range(1)
@@ -436,14 +460,14 @@
     share_range(3)
     start(has_lat_next, *[range_edge(1, other) for other in range(4)])
     start(has_lat_prev, *[range_edge(-1, other) for other in range(4)])
-    send_slices(2)
     arrived(has_lat_prev, lat_halo(1))
     arrived(has_lat_next, lat_halo(-1))
     send_corners()
-    load_its.wait()
-    products([(field4, 3, t) for t in range(OWN_T)], True)
     forward(2)
     send_slices(3)
+    load_its.wait()
+    rows_of_x()
+    first_products()
     step(field3, field4, 1, 2, 1, weights[3], 2, "gather")
     for number in range(4):
         for other in (1, 2, 3):
@@ -469,15 +493,14 @@
     arrived(has_lat_next, *[range_edge(-1, other) for other in range(4)])
     pl.when(has_lat_prev)(lambda: edge_rows(0, -2, 6))
     pl.when(has_lat_next)(lambda: edge_rows(1, OWN, 0))
-    step(field3, field4, 0, 4, 1, weights[3], 2, "join")
-    step(field2, field3, 1, 2, 1, weights[2], 1)
-    products([(field3, 2, t) for t in range(OWN_T)] + [(field2, 1, 1), (field2, 1, 2)], False)
+    step(field3, field4, 0, 4, 1, weights[3], 2, "join", k=2)
+    step(field2, field3, 1, 2, 1, weights[2], 1, k=1)
     wait_slices(2)
     wait_corners(2)
     pl.when(tm > 0)(lambda: step(field3, field4, -1, 1, 1, weights[3], 1))
     pl.when(tm < 15)(lambda: step(field3, field4, OWN_T, 1, 1, weights[3], 1))
-    step(field2, field3, 0, 2, 3, weights[2], 1)
-    products([(field2, 1, 0), (field2, 1, 3)], False)
+    step(field2, field3, 0, 2, 3, weights[2], 1, k=1)
+    products_out()
 
     def sum_y(other):
         target = lax.rem(y + other, 4)
@@ -560,6 +583,8 @@
             vmem(SLICES, ROWS * SEG, 128),
             vmem(SLICES, ROWS * SEG, 128),
             vmem(OWN_T, OWN * SEG, 128),
+            vmem(3 * OWN_T, OWN * SEG, 128),
+            vmem(OWN * SEG, 128),
             vmem(ROWS * SEG, 128),
             vmem(16, OWN, 128),
             vmem(2, 16, 8, 128),

time: 54.4 us -> 51.2 us (0.941)
  the two profiles are of different devices: /device:TPU:6 before, /device:TPU:22 now
where the time goes in v4:
time: 51.2 us; the launch traced here: 51.1 us
  Pallas kernels  49 us (96%)
  local copies, waits for them, and re-layouts  1.39 us (3%)
  between operations  0.64 us (1%)
    pallas_call x1, Pallas kernels, body(): pl.pallas_call(functools.partial(kernel, lats, Sems()), out_shape=(vmem(*...  49 us
    unnamed x2, local copies, waits for them, and re-layouts  1.39 us

profile of v4, /device:TPU:22, one launch (start us, length us, event | category | flops | bytes accessed | tf_op | source)
XLA Modules:
  0.0 51.1 jit_solution(7118638168591786367)
XLA Ops:
  0.6 49.0 %adjoint.1 = (f32[4,16,2048]{2,1,0:T(8,128)S(1)}, f32[16,128]{1,0:T(8,128)S(1)}) custom-call(f32[4,16,2048]{2,1,0:T(8,128)} %cot.1, f32[3,4,16,2048]{3,2,1,0:T(8,128)} %its.1, f32[16,128]{1,0:T(8,128)} %rng.1), custom_call_target="tpu_custom_call" | custom-call | tf_op jit(solution)/shard_map/adjoint/pallas_call | solution.py:571
  49.7 0.8 %copy.7 = f32[4,16,2048]{2,1,0:T(8,128)} copy(f32[4,16,2048]{2,1,0:T(8,128)S(1)} %get-tuple-element.2) | data formatting | bytes 1048576
  50.5 0.6 %copy.8 = f32[16,128]{1,0:T(8,128)} copy(f32[16,128]{1,0:T(8,128)S(1)} %get-tuple-element.3) | data formatting | bytes 16384

commit v5 on v4

--- a/solution.py
+++ b/solution.py
@@ -456,14 +456,14 @@
     arrived(None, range_z(-1))
     share_range(2)
     forward(1)
+    arrived(has_lat_prev, lat_halo(1))
+    arrived(has_lat_next, lat_halo(-1))
+    send_corners()
+    forward(2)
     arrived(None, range_z_second())
     share_range(3)
     start(has_lat_next, *[range_edge(1, other) for other in range(4)])
     start(has_lat_prev, *[range_edge(-1, other) for other in range(4)])
-    arrived(has_lat_prev, lat_halo(1))
-    arrived(has_lat_next, lat_halo(-1))
-    send_corners()
-    forward(2)
     send_slices(3)
     load_its.wait()
     rows_of_x()

time: 51.2 us -> 50.3 us (0.982)
  the two profiles are of different devices: /device:TPU:22 before, /device:TPU:6 now
where the time goes in v5:
time: 50.3 us; the launch traced here: 50.2 us
  Pallas kernels  48.1 us (96%)
  local copies, waits for them, and re-layouts  1.39 us (3%)
  between operations  0.64 us (1%)
    pallas_call x1, Pallas kernels, body(): pl.pallas_call(functools.partial(kernel, lats, Sems()), out_shape=(vmem(*...  48.1 us
    unnamed x2, local copies, waits for them, and re-layouts  1.39 us

profile of v5, /device:TPU:6, one launch (start us, length us, event | category | flops | bytes accessed | tf_op | source)
XLA Modules:
  0.0 50.2 jit_solution(3322249013175447329)
XLA Ops:
  0.6 48.1 %adjoint.1 = (f32[4,16,2048]{2,1,0:T(8,128)S(1)}, f32[16,128]{1,0:T(8,128)S(1)}) custom-call(f32[4,16,2048]{2,1,0:T(8,128)} %cot.1, f32[3,4,16,2048]{3,2,1,0:T(8,128)} %its.1, f32[16,128]{1,0:T(8,128)} %rng.1), custom_call_target="tpu_custom_call" | custom-call | tf_op jit(solution)/shard_map/adjoint/pallas_call | solution.py:571
  48.8 0.8 %copy.7 = f32[4,16,2048]{2,1,0:T(8,128)} copy(f32[4,16,2048]{2,1,0:T(8,128)S(1)} %get-tuple-element.2) | data formatting | bytes 1048576
  49.6 0.6 %copy.8 = f32[16,128]{1,0:T(8,128)} copy(f32[16,128]{1,0:T(8,128)S(1)} %get-tuple-element.3) | data formatting | bytes 16384
